TPU v7x, 32 devices: a whole 2x2x4 slice. The times are simulated.
32 devices in a mesh: dp: 16 (over z, y, x), mp: 2 (over core).
Axes of the slice: x: 2, y: 2, z: 4, core: 2. Of those that a mesh axis runs over, the one named last changes fastest.
Arguments:
- inputs: bfloat16 [16, 1024, 768], P('dp'), may hold values from -6 to 6
- segments: int32 [16, 1024], P('dp'), may hold values from 0 to 28, as said below
- cotangent: bfloat16 [16, 1024, 768], P('dp'), may hold values from -6 to 6
- norm1_gain: float32 [768], replicated, may hold values from 0.5 to 1.5
- norm1_bias: float32 [768], replicated, may hold values from -3 to 3
- qkv_weight: bfloat16 [3, 768, 768], P(None, None, 'mp'), may hold values from -0.21875 to 0.21875
- qv_bias: float32 [2, 768], P(None, 'mp'), may hold values from -3 to 3
- proj_weight: bfloat16 [768, 768], P('mp'), may hold values from -1.75 to 1.75
- proj_bias: float32 [768], replicated, may hold values from -3 to 3
- norm2_gain: float32 [768], replicated, may hold values from 0.5 to 1.5
- norm2_bias: float32 [768], replicated, may hold values from -3 to 3
- fc1_weight: bfloat16 [768, 3072], P(None, 'mp'), may hold values from -0.21875 to 0.21875
- fc1_bias: float32 [3072], P('mp'), may hold values from -3 to 3
- fc2_weight: bfloat16 [3072, 768], P('mp'), may hold values from -0.109375 to 0.109375
- fc2_bias: float32 [768], replicated, may hold values from -3 to 3
Outputs:
- output: bfloat16 [16, 1024, 768], P('dp')
- input_grad: bfloat16 [16, 1024, 768], P('dp')
- norm1_gain_grad: float32 [768], P('dp')
- norm1_bias_grad: float32 [768], P('dp')
- qkv_weight_grad: float32 [3, 768, 768], P(None, 'dp', 'mp')
- qv_bias_grad: float32 [2, 768], P(None, ('mp', 'dp'))
- proj_weight_grad: float32 [768, 768], P('mp', 'dp')
- proj_bias_grad: float32 [768], P('dp')
- norm2_gain_grad: float32 [768], P('dp')
- norm2_bias_grad: float32 [768], P('dp')
- fc1_weight_grad: float32 [768, 3072], P('dp', 'mp')
- fc1_bias_grad: float32 [3072], P(('mp', 'dp'))
- fc2_weight_grad: float32 [3072, 768], P('mp', 'dp')
- fc2_bias_grad: float32 [768], P('dp')
Inputs may be any that keep to these rules, and one draw needn't show every extreme that they name: `segments`: each packed row holds whole images from slot 0 onward, numbered 1, 2, 3 and so on in order, each a run of max(1024 * n // 1024, 1) slots for n one of 576, 400, 256, 225, 144, 100, 64, 36 (patch-size classes of a 240-pixel image); the slots after the last image are 0. One packed row holds only images of the smallest class, as many as fit.
All inputs are finite; a program needn't handle non-finite values.
Results may differ from a plain program's by a relative error of at most 0.013.
Values sent between devices are 32-bit elements; how exact they have to be, the bound alone decides.
No kernel may reach another device: no remote copies, remote signals or barrier semaphores. Data moves between devices by JAX's collectives and lax.ppermute only.
A program may use at most 192 MiB of HBM per device.

v0:
```python
from functools import partial
import jax
import jax.numpy as jnp
from jax import lax
from jax.sharding import PartitionSpec as P

HEAD_DIM = 64
EPSILON = 1e-06
NEG_FILL = -1000000000.0


def layer_norm(values, gain_vec, shift_vec):
    center = values - jnp.mean(values, axis=-1, keepdims=True)
    inv_spread = lax.rsqrt(jnp.mean(center * center, axis=-1, keepdims=True) + EPSILON)
    normed = center * inv_spread
    return (normed * gain_vec + shift_vec, normed, inv_spread)


def norm_back(grad_out, normed, inv_spread, gain_vec):
    scaled = grad_out * gain_vec
    grad_in = inv_spread * (
        scaled
        - jnp.mean(scaled, axis=-1, keepdims=True)
        - normed * jnp.mean(scaled * normed, axis=-1, keepdims=True)
    )
    return (grad_in, jnp.sum(grad_out * normed, axis=0), jnp.sum(grad_out, axis=0))


def product(left_side, right_side):
    return jnp.dot(left_side, right_side, preferred_element_type=jnp.float32)


def row_contract(left_side, right_side):
    return lax.dot_general(
        left_side, right_side, (((0,), (0,)), ((), ())), preferred_element_type=jnp.float32
    )


def back_product(left_side, right_side):
    return lax.dot_general(
        left_side, right_side, (((1,), (1,)), ((), ())), preferred_element_type=jnp.float32
    )


def block_scores(query_block, key_heads, seg_block, seg_row, score_scale):
    scores = (
        jnp.einsum("qhd,khd->hqk", query_block, key_heads, preferred_element_type=jnp.float32)
        * score_scale
    )
    allowed = (seg_block[:, None] == seg_row[None, :]) & (seg_block[:, None] > 0)
    return jnp.where(allowed[None], scores, NEG_FILL)


def row_forward(operands):
    query_row, key_row, value_row, seg_row = operands
    seq_len = query_row.shape[0]
    head_count = query_row.shape[1] // HEAD_DIM
    block_len = min(512, seq_len)
    score_scale = HEAD_DIM ** (-0.5)
    query_heads = query_row.reshape(seq_len, head_count, HEAD_DIM)
    key_heads = key_row.reshape(seq_len, head_count, HEAD_DIM)
    value_heads = value_row.reshape(seq_len, head_count, HEAD_DIM)
    outputs = []
    log_parts = []
    for offset in range(0, seq_len, block_len):
        scores = block_scores(
            query_heads[offset : offset + block_len],
            key_heads,
            seg_row[offset : offset + block_len],
            seg_row,
            score_scale,
        )
        row_max = jnp.max(scores, axis=-1, keepdims=True)
        exponent = jnp.exp(scores - row_max)
        row_total = jnp.sum(exponent, axis=-1, keepdims=True)
        weights = (exponent / row_total).astype(jnp.bfloat16)
        mixed_rows = jnp.einsum(
            "hqk,khd->qhd", weights, value_heads, preferred_element_type=jnp.float32
        )
        outputs.append(mixed_rows.reshape(block_len, head_count * HEAD_DIM))
        log_parts.append((row_max + jnp.log(row_total))[..., 0])
    return (jnp.concatenate(outputs, axis=0), jnp.concatenate(log_parts, axis=1))


def row_backward(operands):
    query_row, key_row, value_row, seg_row, grad_row, log_total = operands
    seq_len = query_row.shape[0]
    head_count = query_row.shape[1] // HEAD_DIM
    block_len = min(512, seq_len)
    score_scale = HEAD_DIM ** (-0.5)
    query_heads = query_row.reshape(seq_len, head_count, HEAD_DIM)
    key_heads = key_row.reshape(seq_len, head_count, HEAD_DIM)
    value_heads = value_row.reshape(seq_len, head_count, HEAD_DIM)
    grad_heads = grad_row.reshape(seq_len, head_count, HEAD_DIM)
    key_grad = jnp.zeros((seq_len, head_count, HEAD_DIM), jnp.float32)
    value_grad = jnp.zeros((seq_len, head_count, HEAD_DIM), jnp.float32)
    query_parts = []
    for offset in range(0, seq_len, block_len):
        query_block = query_heads[offset : offset + block_len]
        grad_block = grad_heads[offset : offset + block_len]
        scores = block_scores(
            query_block, key_heads, seg_row[offset : offset + block_len], seg_row, score_scale
        )
        weights = jnp.exp(scores - log_total[:, offset : offset + block_len, None])
        weights_low = weights.astype(jnp.bfloat16)
        grad_weights = jnp.einsum(
            "qhd,khd->hqk", grad_block, value_heads, preferred_element_type=jnp.float32
        )
        grad_scores = (
            weights * (grad_weights - jnp.sum(weights * grad_weights, axis=-1, keepdims=True))
        ).astype(jnp.bfloat16)
        query_parts.append(
            (
                jnp.einsum(
                    "hqk,khd->qhd", grad_scores, key_heads, preferred_element_type=jnp.float32
                )
                * score_scale
            ).reshape(block_len, head_count * HEAD_DIM)
        )
        key_grad = (
            key_grad
            + jnp.einsum(
                "hqk,qhd->khd", grad_scores, query_block, preferred_element_type=jnp.float32
            )
            * score_scale
        )
        value_grad = value_grad + jnp.einsum(
            "hqk,qhd->khd", weights_low, grad_block, preferred_element_type=jnp.float32
        )
    query_grad = jnp.concatenate(query_parts, axis=0).astype(jnp.bfloat16)
    flat_width = head_count * HEAD_DIM
    return (
        query_grad,
        key_grad.reshape(seq_len, flat_width).astype(jnp.bfloat16),
        value_grad.reshape(seq_len, flat_width).astype(jnp.bfloat16),
    )


def shards(
    inputs,
    segments,
    cotangent,
    norm1_gain,
    norm1_bias,
    qkv_weight,
    qv_bias,
    proj_weight,
    proj_bias,
    norm2_gain,
    norm2_bias,
    fc1_weight,
    fc1_bias,
    fc2_weight,
    fc2_bias,
):
    pack_count, seq_len, model_width = inputs.shape
    row_count = pack_count * seq_len
    local_width = qkv_weight.shape[2]
    row_shape = (pack_count, seq_len, local_width)
    live_rows = (segments > 0).astype(jnp.float32).reshape(row_count, 1)
    flat_in = inputs.reshape(row_count, model_width).astype(jnp.float32)
    norm1_out, norm1_hat, norm1_inv = layer_norm(flat_in, norm1_gain, norm1_bias)
    norm1_low = norm1_out.astype(jnp.bfloat16)
    queries = (product(norm1_low, qkv_weight[0]) + qv_bias[0]).astype(jnp.bfloat16)
    key_rows = product(norm1_low, qkv_weight[1]).astype(jnp.bfloat16)
    value_rows = (product(norm1_low, qkv_weight[2]) + qv_bias[1]).astype(jnp.bfloat16)
    query_packs = queries.reshape(row_shape)
    key_packs = key_rows.reshape(row_shape)
    value_packs = value_rows.reshape(row_shape)
    mixed_rows, log_total = lax.map(row_forward, (query_packs, key_packs, value_packs, segments))
    attended = (mixed_rows.reshape(row_count, local_width) * live_rows).astype(jnp.bfloat16)
    branch = lax.psum(product(attended, proj_weight), "mp") + proj_bias
    middle = flat_in + branch
    norm2_out, norm2_hat, norm2_inv = layer_norm(middle, norm2_gain, norm2_bias)
    norm2_low = norm2_out.astype(jnp.bfloat16)
    hidden = product(norm2_low, fc1_weight) + fc1_bias
    active, gelu_pull = jax.vjp(partial(jax.nn.gelu, approximate=False), hidden)
    active_low = active.astype(jnp.bfloat16)
    result = middle + (lax.psum(product(active_low, fc2_weight), "mp") + fc2_bias)
    output = result.astype(jnp.bfloat16).reshape(pack_count, seq_len, model_width)
    grad_top = cotangent.reshape(row_count, model_width).astype(jnp.float32) * live_rows
    grad_top_low = grad_top.astype(jnp.bfloat16)
    fc2_grad = row_contract(active_low, grad_top_low)
    fc2_bias_grad = jnp.sum(grad_top, axis=0)
    grad_active = back_product(grad_top_low, fc2_weight)
    grad_hidden = gelu_pull(grad_active)[0].astype(jnp.bfloat16)
    fc1_grad = row_contract(norm2_low, grad_hidden)
    fc1_bias_grad = jnp.sum(grad_hidden, axis=0, dtype=jnp.float32)
    grad_norm2 = lax.psum(back_product(grad_hidden, fc1_weight), "mp")
    grad_mid_norm, norm2_gain_grad, norm2_bias_grad = norm_back(
        grad_norm2, norm2_hat, norm2_inv, norm2_gain
    )
    grad_middle = grad_top + grad_mid_norm
    grad_branch = grad_middle.astype(jnp.bfloat16)
    proj_grad = row_contract(attended, grad_branch)
    proj_bias_grad = jnp.sum(grad_branch, axis=0, dtype=jnp.float32)
    grad_attended = back_product(grad_branch, proj_weight).astype(jnp.bfloat16) * live_rows.astype(
        jnp.bfloat16
    )
    query_grad, key_grad, value_grad = lax.map(
        row_backward,
        (
            query_packs,
            key_packs,
            value_packs,
            segments,
            grad_attended.reshape(row_shape),
            log_total,
        ),
    )
    query_grad = query_grad.reshape(row_count, local_width)
    key_grad = key_grad.reshape(row_count, local_width)
    value_grad = value_grad.reshape(row_count, local_width)
    qkv_grad = jnp.stack(
        [
            row_contract(norm1_low, query_grad),
            row_contract(norm1_low, key_grad),
            row_contract(norm1_low, value_grad),
        ]
    )
    qv_bias_grad = jnp.stack(
        [
            jnp.sum(query_grad, axis=0, dtype=jnp.float32),
            jnp.sum(value_grad, axis=0, dtype=jnp.float32),
        ]
    )
    grad_norm1 = lax.psum(
        back_product(query_grad, qkv_weight[0])
        + back_product(key_grad, qkv_weight[1])
        + back_product(value_grad, qkv_weight[2]),
        "mp",
    )
    grad_in_norm, norm1_gain_grad, norm1_bias_grad = norm_back(
        grad_norm1, norm1_hat, norm1_inv, norm1_gain
    )
    input_grad = (
        (grad_middle + grad_in_norm).astype(jnp.bfloat16).reshape(pack_count, seq_len, model_width)
    )
    every_sum = (
        lax.psum_scatter(norm1_gain_grad, "dp", scatter_dimension=0, tiled=True),
        lax.psum_scatter(norm1_bias_grad, "dp", scatter_dimension=0, tiled=True),
        lax.psum_scatter(qkv_grad, "dp", scatter_dimension=1, tiled=True),
        lax.psum_scatter(qv_bias_grad, "dp", scatter_dimension=1, tiled=True),
        lax.psum_scatter(proj_grad, "dp", scatter_dimension=1, tiled=True),
        lax.psum_scatter(proj_bias_grad, "dp", scatter_dimension=0, tiled=True),
        lax.psum_scatter(norm2_gain_grad, "dp", scatter_dimension=0, tiled=True),
        lax.psum_scatter(norm2_bias_grad, "dp", scatter_dimension=0, tiled=True),
        lax.psum_scatter(fc1_grad, "dp", scatter_dimension=0, tiled=True),
        lax.psum_scatter(fc1_bias_grad, "dp", scatter_dimension=0, tiled=True),
        lax.psum_scatter(fc2_grad, "dp", scatter_dimension=1, tiled=True),
        lax.psum_scatter(fc2_bias_grad, "dp", scatter_dimension=0, tiled=True),
    )
    return (
        output,
        input_grad,
        every_sum[0],
        every_sum[1],
        every_sum[2],
        every_sum[3],
        every_sum[4],
        every_sum[5],
        every_sum[6],
        every_sum[7],
        every_sum[8],
        every_sum[9],
        every_sum[10],
        every_sum[11],
    )


def solution(mesh):
    placed = (
        P("dp", None, None),
        P("dp", None),
        P("dp", None, None),
        P(),
        P(),
        P(None, None, "mp"),
        P(None, "mp"),
        P("mp", None),
        P(),
        P(),
        P(),
        P(None, "mp"),
        P("mp"),
        P("mp", None),
        P(),
    )
    return jax.shard_map(
        shards,
        mesh=mesh,
        in_specs=placed,
        out_specs=(
            P("dp", None, None),
            P("dp", None, None),
            P("dp"),
            P("dp"),
            P(None, "dp", "mp"),
            P(None, ("mp", "dp")),
            P("mp", "dp"),
            P("dp"),
            P("dp"),
            P("dp"),
            P("dp", "mp"),
            P(("mp", "dp")),
            P("mp", "dp"),
            P("dp"),
        ),
        check_vma=False,
    )
```

profile of v0, /device:TPU:0, one launch (start us, length us, event | category | flops | bytes accessed | tf_op | source)
XLA Modules:
  0.0 792.5 jit_solution(12064317991579833451)
XLA Ops:
  20.1 2.8 fusion.1
  24.6 3.8 fusion.17
  30.8 2.8 fusion
  35.5 3.8 fusion.16
  43.1 26.1 %all-reduce.14.cloned.1.call-done = f32[1024,768]{1,0:T(8,128)} async-done(((f32[1024,768]{1,0:T(8,128)}), f32[1024,768]{1,0:T(8,128)}) %all-reduce.14.cloned.1.call-update) | async-done | bytes 3145744 | tf_op jit(solution)/shard_map/psum | solution.py:172
  69.2 2.8 fusion.94
  72.9 17.2 %multiply_convert_fusion.2 = (bf16[1024,1536]{1,0:T(8,128)(2,1)}, f32[1024,1536]{1,0:T(8,128)S(1)}, f32[1024,1536]{1,0:T(8,128)S(1)}) fusion(f32[1536]{0:T(1024)S(1)} %copy-done.67, bf16[768,1536]{1,0:T(8,128)(2,1)S(1)} %copy-done, f32[1024,768]{1,0:T(8,128)S(1)} %get-tuple-element.90, f32[768]{0:T(1024)S(1)} %copy-done.68, f32[768]{0:T(1024)S(1)} %copy-done.56, ...), kind=kOutput, calls=%fused_computation.24 | convolution fusion | flops 2523660288 | bytes 21254144 | tf_op jit(solution)/shard_map/dot_general | solution.py:30
  90.1 5.6 convert_reduce_fusion
  97.5 4.3 fusion.102
  103.2 7.0 fusion.101
  110.3 16.2 %all-reduce.16.cloned.1.call-done = f32[1024,768]{1,0:T(8,128)} async-done(((f32[1024,768]{1,0:T(8,128)}), f32[1024,768]{1,0:T(8,128)}) %all-reduce.16.cloned.1.call-update) | async-done | bytes 3145744 | tf_op jit(solution)/shard_map/psum | solution.py:189
  126.5 4.5 multiply_reduce_fusion.2
  131.1 4.3 convert_reduce_fusion.2
  138.8 6.2 multiply_reduce_fusion.1
  145.0 10.0 %multiply_convert_fusion.1 = bf16[6,512,1024]{2,1,0:T(8,128)(2,1)} fusion(f32[6,512,1024]{2,1,0:T(8,128)} %get-tuple-element.108, f32[6,512,1024]{2,1,0:T(8,128)S(1)} %bitcast.153, f32[6,512]{1,0:T(8,128)S(1)} %get-tuple-element.107, f32[6,512]{1,0:T(8,128)S(1)} %log_add_fusion.1), kind=kLoop, calls=%fused_computation.3 | loop fusion | flops 12582912 | bytes 31481856 | tf_op jit(solution)/shard_map/while/body/eval_jaxpr/convert_element_type | solution.py:111
  155.0 5.0 fusion.58
  160.0 4.0 fusion.103
  164.1 3.3 fusion.5
  167.4 7.5 multiply_reduce_fusion
  174.9 5.0 convert_reduce_fusion.3
  179.8 6.6 multiply_convert_fusion
  192.2 2.8 add_add_fusion
  196.1 4.2 fusion.80
  200.4 9.0 %fusion.90 = f32[768,1536]{1,0:T(8,128)} fusion(bf16[1024,1536]{1,0:T(8,128)(2,1)} %copy-done.71, f32[1024,768]{1,0:T(8,128)} %copy-done.4, f32[768]{0:T(1024)S(1)} %copy-done.69, f32[768]{0:T(1024)S(1)} %copy-done.58, f32[1024]{0:T(1024)S(1)} %copy-done.52, f32[1024]{0:T(1024)S(1)} %copy-done.46), kind=kOutput, calls=%fused_computation.149 | convolution fusion | flops 2419851264 | bytes 11024384 | tf_op jit(solution)/shard_map/dot_general | solution.py:34
  209.4 7.6 fusion.60
  228.6 3.1 fusion.31
  231.7 77.2 %all-reduce.8 = (f32[768]{0:T(1024)S(1)}, f32[768]{0:T(1024)S(1)}, f32[2,384]{1,0:T(2,128)S(1)}, f32[768]{0:T(1024)S(1)}, f32[768]{0:T(1024)S(1)}, /*index=5*/f3...) all-reduce(f32[768]{0:T(1024)S(1)} %get-tuple-element.57, ...), channel_id=2, replica_groups=mesh['dp'=16,'mp'=2] {'dp'}, use_global_device_ids=true, to_apply=%region_19.20.clone | all-reduce | flops 6912 | bytes 55296
  313.6 4.6 fusion.42
  321.5 38.5 %reduce-scatter.8.cloned.1.call-done = f32[384,48]{0,1:T(8,128)} async-done(((f32[384,768]{0,1:T(8,128)}), f32[384,48]{0,1:T(8,128)}) %reduce-scatter.8.cloned.1.call-update) | async-done | bytes 73744 | tf_op jit(solution)/shard_map/reduce_scatter | solution.py:244
  360.1 143.2 %reduce-scatter.10.cloned.1.call-done = f32[48,1536]{1,0:T(8,128)} async-done(((f32[768,1536]{1,0:T(8,128)}), f32[48,1536]{1,0:T(8,128)}) %reduce-scatter.10.cloned.1.call-update) | async-done | bytes 294928 | tf_op jit(solution)/shard_map/reduce_scatter | solution.py:248
  503.3 143.0 %reduce-scatter.12.cloned.1.call-done = f32[1536,48]{0,1:T(8,128)} async-done(((f32[1536,768]{0,1:T(8,128)}), f32[1536,48]{0,1:T(8,128)}) %reduce-scatter.12.cloned.1.call-update) | async-done | bytes 294928 | tf_op jit(solution)/shard_map/reduce_scatter | solution.py:250
  646.2 139.2 %reduce-scatter.6.cloned.1.call-done = f32[3,48,384]{2,1,0:T(8,128)} async-done(((f32[3,768,384]{2,1,0:T(8,128)}), f32[3,48,384]{2,1,0:T(8,128)}) %reduce-scatter.6.cloned.1.call-update) | async-done | bytes 221200 | tf_op jit(solution)/shard_map/reduce_scatter | solution.py:242
  (224 shorter events, 53.9 us)
Async XLA Ops:
  7.2 65.4 %copy-start = (bf16[768,1536]{1,0:T(8,128)(2,1)S(1)}, bf16[768,1536]{1,0:T(8,128)(2,1)}, u32[]{:S(2)}) copy-start(bf16[768,1536]{1,0:T(8,128)(2,1)} %param.26) | copy-start | bytes 7077892
  7.2 62.0 %all-reduce.14.cloned.1.call-start = ((), (), s32[]{:S(2)}) async-start(), calls=%async_computation.4 | async-start | bytes 6291456 | tf_op jit(solution)/shard_map/psum | solution.py:172
  8.1 31.2 %copy-start.32 = (f32[1,1024]{1,0:T(1,128)}, f32[1,1024]{1,0:T(1,128)S(1)}, u32[]{:S(2)}) copy-start(f32[1,1024]{1,0:T(1,128)S(1)} %compare_convert_fusion) | copy-start | bytes 12292
  16.1 17.5 %copy-start.15 = (bf16[1024,384]{0,1:T(8,128)(2,1)}, bf16[1024,384]{0,1:T(8,128)(2,1)S(1)}, u32[]{:S(2)}) copy-start(bf16[1024,384]{0,1:T(8,128)(2,1)S(1)} %add_convert_fusion.5) | copy-start | bytes 2359300
  28.4 11.0 %copy-start.18 = (f32[6,64,512]{2,1,0:T(8,128)}, f32[6,64,512]{2,1,0:T(8,128)S(1)}, u32[]{:S(2)}) copy-start(f32[6,64,512]{2,1,0:T(8,128)S(1)} %fusion.17) | copy-start | bytes 2359300
  43.0 83.5 %all-reduce.16.cloned.1.call-start = ((), (), s32[]{:S(2)}) async-start(), calls=%async_computation.5 | async-start | bytes 6291456 | tf_op jit(solution)/shard_map/psum | solution.py:189
  72.1 18.0 %copy-start.4 = (f32[1024,768]{1,0:T(8,128)}, f32[1024,768]{1,0:T(8,128)S(1)}, u32[]{:S(2)}) copy-start(f32[1024,768]{1,0:T(8,128)S(1)} %get-tuple-element.90) | copy-start | bytes 9437188
  72.1 17.9 %copy-start.44 = (f32[1024]{0:T(1024)}, f32[1024]{0:T(1024)S(1)}, u32[]{:S(2)}) copy-start(f32[1024]{0:T(1024)S(1)} %broadcast_multiply_fusion.4) | copy-start | bytes 12292
  72.9 17.2 %copy-start.50 = (f32[1024]{0:T(1024)}, f32[1024]{0:T(1024)S(1)}, u32[]{:S(2)}) copy-start(f32[1024]{0:T(1024)S(1)} %add_rsqrt_fusion) | copy-start | bytes 12292
  72.9 17.2 %copy-start.27 = (bf16[1,1024,768]{2,1,0:T(8,128)(2,1)S(1)}, bf16[1,1024,768]{2,1,0:T(8,128)(2,1)}, u32[]{:S(2)}) copy-start(bf16[1,1024,768]{2,1,0:T(8,128)(2,1)} %param.17) | copy-start | bytes 4718596
  72.9 17.2 %copy-start.33 = (f32[1,1024]{1,0:T(1,128)S(1)}, f32[1,1024]{1,0:T(1,128)}, u32[]{:S(2)}) copy-start(f32[1,1024]{1,0:T(1,128)} %copy-done.32) | copy-start | bytes 12292
  72.9 17.2 %copy-start.66 = (bf16[1536,768]{1,0:T(8,128)(2,1)S(1)}, bf16[1536,768]{1,0:T(8,128)(2,1)}, u32[]{:S(2)}) copy-start(bf16[1536,768]{1,0:T(8,128)(2,1)} %param.28) | copy-start | bytes 7077892
  101.9 126.7 %all-reduce.18.cloned.1.call-start = ((), (), s32[]{:S(2)}) async-start(), calls=%async_computation.10 | async-start | bytes 12582912 | tf_op jit(solution)/shard_map/psum | solution.py:179
  103.2 23.3 %copy-start.45 = (f32[1024]{0:T(1024)S(1)}, f32[1024]{0:T(1024)}, u32[]{:S(2)}) copy-start(f32[1024]{0:T(1024)} %copy-done.44) | copy-start | bytes 12292
  103.2 23.3 %copy-start.51 = (f32[1024]{0:T(1024)S(1)}, f32[1024]{0:T(1024)}, u32[]{:S(2)}) copy-start(f32[1024]{0:T(1024)} %copy-done.50) | copy-start | bytes 12292
  103.2 23.3 %copy-start.57 = (f32[768]{0:T(1024)S(1)}, f32[768]{0:T(1024)}, u32[]{:S(2)}) copy-start(f32[768]{0:T(1024)} %param.24) | copy-start | bytes 9220
  110.3 20.8 %copy-start.28 = (bf16[1,1024,768]{2,1,0:T(8,128)(2,1)S(1)}, bf16[1,1024,768]{2,1,0:T(8,128)(2,1)}, u32[]{:S(2)}) copy-start(bf16[1,1024,768]{2,1,0:T(8,128)(2,1)} %param.17) | copy-start | bytes 4718596
  126.5 12.3 %slice-start = ((s8[12582912]{0:T(1024)(128)(4,1)}), s8[4194304]{0:T(1024)(128)(4,1)S(1)}, s32[]{:S(2)}) async-start(s8[12582912]{0:T(1024)(128)(4,1)} %bitcast.152), calls=%async_computation.11 | async-start | bytes 8388608
  131.0 7.7 slice-start.1
  131.1 7.7 slice-start.2
  145.0 19.0 %slice-start.3 = ((s8[12582912]{0:T(1024)(128)(4,1)}), s8[4194304]{0:T(1024)(128)(4,1)S(1)}, s32[]{:S(2)}) async-start(s8[12582912]{0:T(1024)(128)(4,1)} %bitcast.154), calls=%async_computation.14 | async-start | bytes 8388608
  145.0 19.0 %slice-start.4 = ((s8[12582912]{0:T(1024)(128)(4,1)}), s8[4194304]{0:T(1024)(128)(4,1)S(1)}, s32[]{:S(2)}) async-start(s8[12582912]{0:T(1024)(128)(4,1)} %bitcast.154), calls=%async_computation.15 | async-start | bytes 8388608
  155.0 9.0 %slice-start.5 = ((s8[12582912]{0:T(1024)(128)(4,1)}), s8[4194304]{0:T(1024)(128)(4,1)S(1)}, s32[]{:S(2)}) async-start(s8[12582912]{0:T(1024)(128)(4,1)} %bitcast.154), calls=%async_computation.16 | async-start | bytes 8388608
  195.0 165.1 %reduce-scatter.8.cloned.1.call-start = ((), (), s32[]{:S(2)}) async-start(), calls=%async_computation.7 | async-start | bytes 1253376 | tf_op jit(solution)/shard_map/reduce_scatter | solution.py:244
  200.3 303.0 %reduce-scatter.10.cloned.1.call-start = ((), (), s32[]{:S(2)}) async-start(), calls=%async_computation.8 | async-start | bytes 5013504 | tf_op jit(solution)/shard_map/reduce_scatter | solution.py:248
  209.4 436.8 %reduce-scatter.12.cloned.1.call-start = ((), (), s32[]{:S(2)}) async-start(), calls=%async_computation.9 | async-start | bytes 5013504 | tf_op jit(solution)/shard_map/reduce_scatter | solution.py:250
  217.0 568.4 %reduce-scatter.6.cloned.1.call-start = ((), (), s32[]{:S(2)}) async-start(), calls=%async_computation.6 | async-start | bytes 3760128 | tf_op jit(solution)/shard_map/reduce_scatter | solution.py:242
  225.1 6.6 copy-start.53
  225.1 6.6 copy-start.54
  225.1 6.6 copy-start.59
  225.1 88.5 %copy-start.62 = (f32[768]{0:T(1024)S(1)}, f32[768]{0:T(1024)}, u32[]{:S(2)}) copy-start(f32[768]{0:T(1024)} %param.29) | copy-start | bytes 9220
  313.6 471.8 %copy-start.1 = (bf16[768,1536]{1,0:T(8,128)(2,1)S(1)}, bf16[768,1536]{1,0:T(8,128)(2,1)}, u32[]{:S(2)}) copy-start(bf16[768,1536]{1,0:T(8,128)(2,1)} %param.26) | copy-start | bytes 7077892
  (53 other events, 170.4 us)
Sparse Core Ops, SparseCore 0:
  43.1 26.0 all-reduce.13
  102.0 24.4 all-reduce.15
  195.1 33.4 all-reduce.17
  233.7 126.2 reduce-scatter.7
  365.6 137.5 reduce-scatter.9
  508.8 137.3 reduce-scatter.11
  651.9 133.4 reduce-scatter.5
where the time goes:
time: 796 us; the launch traced here: 792 us
  waiting for transfers between devices  506 us (64%)
  matrix products  117 us (15%)
  blocking collectives  77.2 us (10%)
  other arithmetic  53.9 us (7%)
  local copies, waits for them, and re-layouts  19.7 us (2%)
  between operations  17.3 us (2%)
    reduce_scatter x1, waiting for transfers between devices, shards(): lax.psum_scatter(fc1_grad, 'dp', scatter_dimension=0, tiled=True)  143 us
    reduce_scatter x1, waiting for transfers between devices, shards(): lax.psum_scatter(fc2_grad, 'dp', scatter_dimension=1, tiled=True)  143 us
    reduce_scatter x1, waiting for transfers between devices, shards(): lax.psum_scatter(qkv_grad, 'dp', scatter_dimension=1, tiled=True)  139 us
    unnamed x1, blocking collectives  77.2 us
    reduce_scatter x1, waiting for transfers between devices, shards(): lax.psum_scatter(proj_grad, 'dp', scatter_dimension=1, tiled=True)  38.5 us
    dot_general x6, matrix products, product(): return jnp.dot(left_side, right_side, preferred_element_type=jnp.float32)  29.4 us
    psum x1, waiting for transfers between devices, shards(): branch = lax.psum(product(attended, proj_weight), 'mp') + proj_bias  26.1 us
    dot_general x6, matrix products, row_contract(): lax.dot_general(left_side, right_side, (((0,), (0,)), ((), ())), preferre...  25.8 us
  transfers between devices with their start and end apart: 7, of which 6 were waited for; matrix products, arithmetic and copies ran while one was open for 6% of the time, Pallas kernels for 0%

commit v1 on v0

--- a/solution.py
+++ b/solution.py
@@ -186,7 +186,7 @@
     grad_hidden = gelu_pull(grad_active)[0].astype(jnp.bfloat16)
     fc1_grad = row_contract(norm2_low, grad_hidden)
     fc1_bias_grad = jnp.sum(grad_hidden, axis=0, dtype=jnp.float32)
-    grad_norm2 = lax.psum(back_product(grad_hidden, fc1_weight), "mp")
+    grad_norm2 = jnp.sum(lax.all_gather(back_product(grad_hidden, fc1_weight), "mp"), axis=0)
     grad_mid_norm, norm2_gain_grad, norm2_bias_grad = norm_back(
         grad_norm2, norm2_hat, norm2_inv, norm2_gain
     )

time: 796 us -> 795 us (level)
  waiting for transfers between devices: 506 us -> 497 us
  other arithmetic: 53.9 us -> 62.3 us
    psum x1 -> x0, waiting for transfers between devices: 16.2 us -> none  [shards(): grad_norm2 = lax.psum(back_product(grad_hidden, fc1_weight), 'mp')]
    all_gather x0 -> x1, waiting for transfers between devices: none -> 9.79 us  [shards(): lax.all_gather(back_product(grad_hidden, fc1_weight), 'mp')]
    reduce_sum x0 -> x2, other arithmetic: none -> 8.45 us  [the longest x1 5.23 us: shards(): jnp.sum(lax.all_gather(back_product(grad_hidden, fc1_weight), 'mp'), axis=0)]
    unnamed x165 -> x163, local copies, waits for them, and re-layouts: 17.9 us -> 17.8 us
  transfers between devices with their start and end apart: 7 -> 7, of which waited for: 6 -> 6; matrix products, arithmetic and copies ran while one was open for 6% -> 7% of each run, Pallas kernels for 0% -> 0%
where the time goes in v1:
time: 795 us; the launch traced here: 791 us
  waiting for transfers between devices  497 us (63%)
  matrix products  117 us (15%)
  blocking collectives  77.2 us (10%)
  other arithmetic  62.3 us (8%)
  local copies, waits for them, and re-layouts  19.6 us (2%)
  between operations  17.2 us (2%)
    reduce_scatter x1, waiting for transfers between devices, shards(): lax.psum_scatter(fc2_grad, 'dp', scatter_dimension=1, tiled=True)  143 us
    reduce_scatter x1, waiting for transfers between devices, shards(): lax.psum_scatter(fc1_grad, 'dp', scatter_dimension=0, tiled=True)  143 us
    reduce_scatter x1, waiting for transfers between devices, shards(): lax.psum_scatter(qkv_grad, 'dp', scatter_dimension=1, tiled=True)  139 us
    unnamed x1, blocking collectives  77.2 us
    reduce_scatter x1, waiting for transfers between devices, shards(): lax.psum_scatter(proj_grad, 'dp', scatter_dimension=1, tiled=True)  35.4 us
    dot_general x6, matrix products, product(): return jnp.dot(left_side, right_side, preferred_element_type=jnp.float32)  29.4 us
    psum x1, waiting for transfers between devices, shards(): branch = lax.psum(product(attended, proj_weight), 'mp') + proj_bias  26.1 us
    dot_general x6, matrix products, row_contract(): lax.dot_general(left_side, right_side, (((0,), (0,)), ((), ())), preferre...  25.8 us
  transfers between devices with their start and end apart: 7, of which 6 were waited for; matrix products, arithmetic and copies ran while one was open for 7% of the time, Pallas kernels for 0%

profile of v1, /device:TPU:0, one launch (start us, length us, event | category | flops | bytes accessed | tf_op | source)
XLA Modules:
  0.0 791.4 jit_solution(13417159309625524121)
XLA Ops:
  20.1 2.8 fusion.1
  24.6 3.8 fusion.17
  35.5 3.8 fusion.16
  43.0 26.1 %all-reduce.13.cloned.1.call-done = f32[1024,768]{1,0:T(8,128)} async-done(((f32[1024,768]{1,0:T(8,128)}), f32[1024,768]{1,0:T(8,128)}) %all-reduce.13.cloned.1.call-update) | async-done | bytes 3145744 | tf_op jit(solution)/shard_map/psum | solution.py:172
  69.2 2.8 fusion.94
  72.8 17.2 %multiply_convert_fusion.2 = (bf16[1024,1536]{1,0:T(8,128)(2,1)}, f32[1024,1536]{1,0:T(8,128)S(1)}, f32[1024,1536]{1,0:T(8,128)S(1)}) fusion(f32[1536]{0:T(1024)S(1)} %copy-done.66, bf16[768,1536]{1,0:T(8,128)(2,1)S(1)} %copy-done, f32[1024,768]{1,0:T(8,128)S(1)} %get-tuple-element.89, f32[768]{0:T(1024)S(1)} %copy-done.67, f32[768]{0:T(1024)S(1)} %copy-done.53, ...), kind=kOutput, calls=%fused_computation.24 | convolution fusion | flops 2523660288 | bytes 21254144 | tf_op jit(solution)/shard_map/dot_general | solution.py:30
  90.1 5.6 convert_reduce_fusion
  97.4 4.3 fusion.102
  103.0 7.0 fusion.101
  110.0 9.8 %all-gather.3.cloned.1.call-done = f32[2048,768]{1,0:T(8,128)} async-done(((f32[1024,768]{1,0:T(8,128)}), f32[2048,768]{1,0:T(8,128)}) %all-gather.3.cloned.1.call-update) | async-done | bytes 6291472 | tf_op jit(solution)/shard_map/all_gather | solution.py:189
  119.8 5.2 reduce_sum.208
  125.1 4.5 multiply_reduce_fusion.2
  129.6 4.3 convert_reduce_fusion.2
  137.3 6.2 multiply_reduce_fusion.1
  143.5 10.1 %multiply_convert_fusion.1 = bf16[6,512,1024]{2,1,0:T(8,128)(2,1)} fusion(f32[6,512,1024]{2,1,0:T(8,128)} %get-tuple-element.107, f32[6,512,1024]{2,1,0:T(8,128)S(1)} %bitcast.154, f32[6,512]{1,0:T(8,128)S(1)} %get-tuple-element.106, f32[6,512]{1,0:T(8,128)S(1)} %log_add_fusion.1), kind=kLoop, calls=%fused_computation.3 | loop fusion | flops 12582912 | bytes 31481856 | tf_op jit(solution)/shard_map/while/body/eval_jaxpr/convert_element_type | solution.py:111
  153.6 5.0 fusion.58
  158.5 4.0 fusion.103
  162.6 3.3 fusion.5
  165.9 7.5 multiply_reduce_fusion
  173.4 5.0 convert_reduce_fusion.3
  178.3 6.6 multiply_convert_fusion
  194.5 4.2 fusion.80
  198.8 9.0 %fusion.90 = f32[768,1536]{1,0:T(8,128)} fusion(bf16[1024,1536]{1,0:T(8,128)(2,1)} %copy-done.70, f32[1024,768]{1,0:T(8,128)} %copy-done.4, f32[768]{0:T(1024)S(1)} %copy-done.68, f32[768]{0:T(1024)S(1)} %copy-done.55, f32[1024]{0:T(1024)S(1)} %copy-done.49, f32[1024]{0:T(1024)S(1)} %copy-done.40), kind=kOutput, calls=%fused_computation.149 | convolution fusion | flops 2419851264 | bytes 11024384 | tf_op jit(solution)/shard_map/dot_general | solution.py:34
  207.8 7.6 fusion.60
  226.9 3.2 reduce_sum.221
  230.2 3.1 fusion.31
  233.3 77.2 %all-reduce.8 = (f32[768]{0:T(1024)S(1)}, f32[768]{0:T(1024)S(1)}, f32[2,384]{1,0:T(2,128)S(1)}, f32[768]{0:T(1024)S(1)}, f32[768]{0:T(1024)S(1)}, /*index=5*/f3...) all-reduce(f32[768]{0:T(1024)S(1)} %get-tuple-element.57, ...), channel_id=3, replica_groups=mesh['dp'=16,'mp'=2] {'dp'}, use_global_device_ids=true, to_apply=%region_19.20.clone | all-reduce | flops 6912 | bytes 55296
  315.3 4.6 fusion.42
  323.1 35.4 %reduce-scatter.8.cloned.1.call-done = f32[384,48]{0,1:T(8,128)} async-done(((f32[384,768]{0,1:T(8,128)}), f32[384,48]{0,1:T(8,128)}) %reduce-scatter.8.cloned.1.call-update) | async-done | bytes 73744 | tf_op jit(solution)/shard_map/reduce_scatter | solution.py:244
  358.5 143.2 %reduce-scatter.10.cloned.1.call-done = f32[48,1536]{1,0:T(8,128)} async-done(((f32[768,1536]{1,0:T(8,128)}), f32[48,1536]{1,0:T(8,128)}) %reduce-scatter.10.cloned.1.call-update) | async-done | bytes 294928 | tf_op jit(solution)/shard_map/reduce_scatter | solution.py:248
  501.7 143.3 %reduce-scatter.12.cloned.1.call-done = f32[1536,48]{0,1:T(8,128)} async-done(((f32[1536,768]{0,1:T(8,128)}), f32[1536,48]{0,1:T(8,128)}) %reduce-scatter.12.cloned.1.call-update) | async-done | bytes 294928 | tf_op jit(solution)/shard_map/reduce_scatter | solution.py:250
  645.0 139.3 %reduce-scatter.6.cloned.1.call-done = f32[3,48,384]{2,1,0:T(8,128)} async-done(((f32[3,768,384]{2,1,0:T(8,128)}), f32[3,48,384]{2,1,0:T(8,128)}) %reduce-scatter.6.cloned.1.call-update) | async-done | bytes 221200 | tf_op jit(solution)/shard_map/reduce_scatter | solution.py:242
  (224 shorter events, 59.2 us)
Async XLA Ops:
  7.2 65.4 %copy-start = (bf16[768,1536]{1,0:T(8,128)(2,1)S(1)}, bf16[768,1536]{1,0:T(8,128)(2,1)}, u32[]{:S(2)}) copy-start(bf16[768,1536]{1,0:T(8,128)(2,1)} %param.26) | copy-start | bytes 7077892
  7.2 5.6 copy-start.64
  7.2 5.6 copy-start.51
  7.2 5.6 copy-start.62
  7.2 61.9 %all-reduce.13.cloned.1.call-start = ((), (), s32[]{:S(2)}) async-start(), calls=%async_computation.4 | async-start | bytes 6291456 | tf_op jit(solution)/shard_map/psum | solution.py:172
  7.3 5.6 copy-start.5
  8.1 31.2 %copy-start.32 = (f32[1,1024]{1,0:T(1,128)}, f32[1,1024]{1,0:T(1,128)S(1)}, u32[]{:S(2)}) copy-start(f32[1,1024]{1,0:T(1,128)S(1)} %compare_convert_fusion) | copy-start | bytes 12292
  16.1 17.5 %copy-start.15 = (bf16[1024,384]{0,1:T(8,128)(2,1)}, bf16[1024,384]{0,1:T(8,128)(2,1)S(1)}, u32[]{:S(2)}) copy-start(bf16[1024,384]{0,1:T(8,128)(2,1)S(1)} %add_convert_fusion.5) | copy-start | bytes 2359300
  22.9 5.5 copy-start.41
  28.4 11.0 %copy-start.18 = (f32[6,64,512]{2,1,0:T(8,128)}, f32[6,64,512]{2,1,0:T(8,128)S(1)}, u32[]{:S(2)}) copy-start(f32[6,64,512]{2,1,0:T(8,128)S(1)} %fusion.17) | copy-start | bytes 2359300
  43.0 76.8 %all-gather.3.cloned.1.call-start = ((), (), s32[]{:S(2)}) async-start(), calls=%async_computation.9 | async-start | bytes 9437184 | tf_op jit(solution)/shard_map/all_gather | solution.py:189
  72.0 18.0 %copy-start.4 = (f32[1024,768]{1,0:T(8,128)}, f32[1024,768]{1,0:T(8,128)S(1)}, u32[]{:S(2)}) copy-start(f32[1024,768]{1,0:T(8,128)S(1)} %get-tuple-element.89) | copy-start | bytes 9437188
  72.1 18.0 %copy-start.38 = (f32[1024]{0:T(1024)}, f32[1024]{0:T(1024)S(1)}, u32[]{:S(2)}) copy-start(f32[1024]{0:T(1024)S(1)} %broadcast_multiply_fusion.4) | copy-start | bytes 12292
  72.8 17.2 %copy-start.47 = (f32[1024]{0:T(1024)}, f32[1024]{0:T(1024)S(1)}, u32[]{:S(2)}) copy-start(f32[1024]{0:T(1024)S(1)} %add_rsqrt_fusion) | copy-start | bytes 12292
  72.8 17.2 %copy-start.27 = (bf16[1,1024,768]{2,1,0:T(8,128)(2,1)S(1)}, bf16[1,1024,768]{2,1,0:T(8,128)(2,1)}, u32[]{:S(2)}) copy-start(bf16[1,1024,768]{2,1,0:T(8,128)(2,1)} %param.17) | copy-start | bytes 4718596
  72.8 17.2 %copy-start.33 = (f32[1,1024]{1,0:T(1,128)S(1)}, f32[1,1024]{1,0:T(1,128)}, u32[]{:S(2)}) copy-start(f32[1,1024]{1,0:T(1,128)} %copy-done.32) | copy-start | bytes 12292
  72.8 17.2 %copy-start.65 = (bf16[1536,768]{1,0:T(8,128)(2,1)S(1)}, bf16[1536,768]{1,0:T(8,128)(2,1)}, u32[]{:S(2)}) copy-start(bf16[1536,768]{1,0:T(8,128)(2,1)} %param.28) | copy-start | bytes 7077892
  101.7 128.5 %all-reduce.15.cloned.1.call-start = ((), (), s32[]{:S(2)}) async-start(), calls=%async_computation.10 | async-start | bytes 12582912 | tf_op jit(solution)/shard_map/psum | solution.py:179
  125.1 12.2 %slice-start = ((s8[12582912]{0:T(1024)(128)(4,1)}), s8[4194304]{0:T(1024)(128)(4,1)S(1)}, s32[]{:S(2)}) async-start(s8[12582912]{0:T(1024)(128)(4,1)} %bitcast.153), calls=%async_computation.11 | async-start | bytes 8388608
  129.6 6.0 copy-start.22
  129.6 7.7 slice-start.1
  129.6 7.7 slice-start.2
  143.5 19.1 %slice-start.3 = ((s8[12582912]{0:T(1024)(128)(4,1)}), s8[4194304]{0:T(1024)(128)(4,1)S(1)}, s32[]{:S(2)}) async-start(s8[12582912]{0:T(1024)(128)(4,1)} %bitcast.155), calls=%async_computation.14 | async-start | bytes 8388608
  143.5 19.1 %slice-start.4 = ((s8[12582912]{0:T(1024)(128)(4,1)}), s8[4194304]{0:T(1024)(128)(4,1)S(1)}, s32[]{:S(2)}) async-start(s8[12582912]{0:T(1024)(128)(4,1)} %bitcast.155), calls=%async_computation.15 | async-start | bytes 8388608
  153.5 9.0 %slice-start.5 = ((s8[12582912]{0:T(1024)(128)(4,1)}), s8[4194304]{0:T(1024)(128)(4,1)S(1)}, s32[]{:S(2)}) async-start(s8[12582912]{0:T(1024)(128)(4,1)} %bitcast.155), calls=%async_computation.16 | async-start | bytes 8388608
  193.4 165.1 %reduce-scatter.8.cloned.1.call-start = ((), (), s32[]{:S(2)}) async-start(), calls=%async_computation.6 | async-start | bytes 1253376 | tf_op jit(solution)/shard_map/reduce_scatter | solution.py:244
  198.7 303.0 %reduce-scatter.10.cloned.1.call-start = ((), (), s32[]{:S(2)}) async-start(), calls=%async_computation.7 | async-start | bytes 5013504 | tf_op jit(solution)/shard_map/reduce_scatter | solution.py:248
  207.8 437.2 %reduce-scatter.12.cloned.1.call-start = ((), (), s32[]{:S(2)}) async-start(), calls=%async_computation.8 | async-start | bytes 5013504 | tf_op jit(solution)/shard_map/reduce_scatter | solution.py:250
  215.4 568.9 %reduce-scatter.6.cloned.1.call-start = ((), (), s32[]{:S(2)}) async-start(), calls=%async_computation.5 | async-start | bytes 3760128 | tf_op jit(solution)/shard_map/reduce_scatter | solution.py:242
  230.2 85.0 %copy-start.61 = (f32[768]{0:T(1024)S(1)}, f32[768]{0:T(1024)}, u32[]{:S(2)}) copy-start(f32[768]{0:T(1024)} %param.29) | copy-start | bytes 9220
  315.2 5.8 copy-start.10
  315.2 469.1 %copy-start.1 = (bf16[768,1536]{1,0:T(8,128)(2,1)S(1)}, bf16[768,1536]{1,0:T(8,128)(2,1)}, u32[]{:S(2)}) copy-start(bf16[768,1536]{1,0:T(8,128)(2,1)} %param.26) | copy-start | bytes 7077892
  (52 other events, 150.0 us)
Sparse Core Ops, SparseCore 0:
  43.1 26.0 all-reduce.12
  101.8 17.9 all-gather.2
  193.5 33.4 all-reduce.14
  232.1 126.3 reduce-scatter.7
  364.1 137.5 reduce-scatter.9
  507.3 137.7 reduce-scatter.11
  650.7 133.5 reduce-scatter.5
